TPU v7x, 32 devices: a whole 2x2x4 slice. The times are simulated.
32 devices in a mesh: scene: 8 (over z, x), tie: 4 (over y, core).
Axes of the slice: x: 2, y: 2, z: 4, core: 2. Of those that a mesh axis runs over, the one named last changes fastest.
Arguments:
- tie_rows: bfloat16 [384, 256, 256], P('tie'), may hold values from -0.375 to 0.375
- point_counts: int32 [384], P('tie'), may hold values from 1 to 128, as said below
- pattern: int32 [128, 384], P('scene', 'tie'), may hold values 0 or 1
- sensitivity: bfloat16 [128, 192, 192], P('scene'), may hold values from -0.119628906 to 0.119628906
- damping: float32 [128], P(('scene', 'tie')), may hold values from 1 to 8
- prior: float32 [64], replicated, may hold values from 0.25 to 4
Outputs:
- scene_rows: float32 [128, 192, 256], P(('scene', 'tie'))
- global_factor: float32 [64, 64], replicated
Inputs may be any that keep to these rules, and one draw needn't show every extreme that they name: `point_counts`: points present in each block; some block is full.
All inputs are finite; a program needn't handle non-finite values. No bound on the sum of `pattern` on one device may be relied on, other than what follows from the above.
Results may differ from a plain program's by a relative error of at most 0.0003.
Values sent between devices are 32-bit elements; how exact they have to be, the bound alone decides.
A program may use at most 128 MiB of HBM per device.

v0:
```python
import functools

import jax
import jax.numpy as jnp
from jax import lax
from jax.experimental import pallas as pl
from jax.experimental.pallas import tpu as pltpu
from jax.sharding import PartitionSpec as P


MESH = pl.DeviceIdType.MESH
F32 = jnp.float32
BF16 = jnp.bfloat16
PANEL = 32
LANES = 128
SUB = 8
UNROLL = 8
DEPTH = 32
PIECES = 2
VMEM = pl.BlockSpec(memory_space=pltpu.VMEM)


def over_rows(a, b):
    return lax.dot_general(a, b, (((0,), (0,)), ((), ())), preferred_element_type=F32)


def gram_kernel(groups, own, pairs, counts, pattern, rows, *rest):
    outs = rest[: len(groups)]
    ring, acc, entries, arrived = rest[len(groups) :]
    depth, _, wide = ring.shape
    half = wide // 2
    total = pattern.shape[1]
    stride = 1 << (total - 1).bit_length()
    me = lax.axis_index("tie")

    def fetch(n):
        at = lax.rem(n, depth)
        block = entries[n] & (stride - 1)
        return pltpu.make_async_copy(rows.at[block], ring.at[at], arrived.at[at])

    def start_fetch(n, carry):
        fetch(n).start()
        return carry

    filled = jnp.int32(0)
    place = 0
    for hop, side, offset, size in groups:
        device = lax.rem(me // 2 + hop, pairs) * 2 + lax.rem(me + side, 2)

        def scan(q, n, device=device, offset=offset, place=place):
            scene = device * own + offset + q
            base = (place + q) * stride
            was = n
            for block in range(total):
                entries[n] = base + block
                n = n + pattern[scene, block]
            lax.fori_loop(jnp.minimum(was, depth), jnp.minimum(n, depth), start_fetch, 0)
            return n

        filled = lax.fori_loop(0, size, scan, filled)
        place += size
    acc[...] = jnp.zeros_like(acc)
    reach = lax.broadcasted_iota(jnp.int32, (2 * SUB, wide), 1)

    def step(it, carry):
        for u in range(UNROLL):
            n = it * UNROLL + u

            @pl.when(n < filled)
            def _(n=n):
                fetch(n).wait()

        for u in range(UNROLL):
            n = it * UNROLL + u
            at = jnp.minimum(n, filled - 1)
            entry = entries[at]
            keep = jnp.where(n < filled, 2 * counts[entry & (stride - 1)], 0)
            value = ring[lax.rem(at, depth)]
            mask = jnp.where(reach < keep, 1.0, 0.0).astype(BF16)
            kept = value.T * jnp.concatenate([mask] * (wide // (2 * SUB)), 0)
            top = jnp.dot(kept[:half], value, preferred_element_type=F32)
            bottom = jnp.dot(kept[half:], value[:, half:], preferred_element_type=F32)
            to = entry // stride
            acc[to, :half] += top[:, :half]
            acc[to, half : 2 * half] += top[:, half:]
            acc[to, 2 * half :] += bottom
        for u in range(UNROLL):
            n = it * UNROLL + u + depth

            @pl.when(n < filled)
            def _(n=n):
                fetch(n).start()

        return carry

    lax.fori_loop(0, (filled + UNROLL - 1) // UNROLL, step, 0)
    row = lax.broadcasted_iota(jnp.int32, (half, half), 0)
    lane = lax.broadcasted_iota(jnp.int32, (half, half), 1)
    place = 0
    for out, (_, _, _, size) in zip(outs, groups):
        diagonals = [None] * size
        for q in range(size):
            low = acc[place, 2 * half :]
            at = q * wide
            out[at : at + half] = acc[place, half : 2 * half]
            out[at + half : at + wide] = jnp.where(row <= lane, acc[place, :half], low)
            diagonals[q] = jnp.sum(jnp.where(row == lane, low, 0.0), 0, keepdims=True)
            place += 1
        diagonals += [jnp.zeros((1, half), F32)] * (out.shape[0] - size * wide - size)
        out[size * wide :] = jnp.concatenate(diagonals, 0)


def gram_sums(tie_rows, point_counts, pattern, groups, own, n):
    total, height, wide = tie_rows.shape
    half = wide // 2
    sizes = [group[3] for group in groups]
    most = sum(sizes)
    smem = pl.BlockSpec(memory_space=pltpu.SMEM)
    return pl.pallas_call(
        functools.partial(gram_kernel, groups, own, n // 2),
        in_specs=[smem, smem, pl.BlockSpec(memory_space=pl.ANY)],
        out_specs=[VMEM] * len(sizes),
        out_shape=[
            jax.ShapeDtypeStruct((size * wide + -(-size // SUB) * SUB, half), F32) for size in sizes
        ],
        scratch_shapes=[
            pltpu.VMEM((DEPTH, height, wide), BF16),
            pltpu.VMEM((most, 3 * half, half), F32),
            pltpu.SMEM((most * total + 1,), jnp.int32),
            pltpu.SemaphoreType.DMA((DEPTH,)),
        ],
        compiler_params=pltpu.CompilerParams(vmem_limit_bytes=16 << 20),
    )(point_counts, pattern, tie_rows)


def join_kernel(x, y, out):
    out[...] = x[...] + y[...]


def join(x, y):
    return pl.pallas_call(
        join_kernel,
        in_specs=[VMEM] * 2,
        out_specs=VMEM,
        out_shape=jax.ShapeDtypeStruct(x.shape, F32),
        compiler_params=pltpu.CompilerParams(vmem_limit_bytes=4 << 20),
        name="join",
    )(x, y)


def swap_cores(x, n):
    return lax.ppermute(x, "tie", [(t, t ^ 1) for t in range(n)])


def send_over(x, n, hop):
    pairs = n // 2
    return lax.ppermute(x, "tie", [(t, (t // 2 + hop) % pairs * 2 + t % 2) for t in range(n)])


def merged_sums(tie_rows, point_counts, pattern, own, n):
    size = own // PIECES
    parts = []
    tie_rows, point_counts, pattern = (
        pltpu.with_memory_space_constraint(x, pltpu.HBM) for x in (tie_rows, point_counts, pattern)
    )
    for hop in range(1, n // 2):
        for offset in range(0, own, size):
            groups = [(hop, side, offset, size) for side in (1, 0)]
            theirs, mine = gram_sums(tie_rows, point_counts, pattern, groups, own, n)
            both = join(mine, swap_cores(theirs, n))
            both, point_counts = lax.optimization_barrier((both, point_counts))
            parts.append((offset, send_over(both, n, hop)))
    groups = [(0, 1, 0, own), (0, 0, 0, own)]
    theirs, mine = gram_sums(tie_rows, point_counts, pattern, groups, own, n)
    return [(0, mine), (0, swap_cores(theirs, n))] + parts


def two_parts(x):
    high = x.astype(BF16)
    return high, (x - high.astype(F32)).astype(BF16)


def eliminate(panels, first):
    height, wide = panels[0].shape
    tile = (SUB, LANES)
    count = height // SUB
    rows = [[p[SUB * h : SUB * (h + 1)] for h in range(count)] for p in panels]
    row_index = lax.broadcasted_iota(jnp.int32, (SUB, wide), 0)
    lane = lax.broadcasted_iota(jnp.int32, (SUB, wide), 1)
    tile_row = lax.broadcasted_iota(jnp.int32, tile, 0)
    below = [tile_row > k for k in range(SUB)]

    def spread(x):
        return x if wide == LANES else (jnp.concatenate([x] * (wide // LANES), 1) if wide > LANES else x[:, :wide])

    for g in range(count):
        start = first + SUB * g
        cols = [
            [[jnp.broadcast_to(r[h][:, start + m : start + m + 1], tile) for h in range(g, count)] for m in range(SUB)]
            for r in rows
        ]
        for q, r in enumerate(rows):
            b = cols[q]
            pivots = b[0][0]
            for k in range(SUB):
                inverse = 1.0 / b[k][0][k : k + 1]
                pivots = jnp.where(tile_row == k, b[k][0], pivots)
                scaled = r[g][k : k + 1] * spread(inverse)
                factors = [b[m][0][k : k + 1] * inverse for m in range(k + 1, SUB)]
                for h in range(g, count):
                    column = b[k][h - g]
                    if h == g:
                        if k == SUB - 1:
                            continue
                        column = jnp.where(below[k], column, 0.0)
                    for m in range(k + 1, SUB):
                        b[m][h - g] = b[m][h - g] - column * factors[m - k - 1]
                    r[h] = r[h] - spread(column) * scaled
            r[g] = jnp.where(lane >= row_index + start, r[g] * spread(lax.rsqrt(pivots)), 0.0)
    return rows


def exchange(ref, slots, send, recv, name, n, width=None):
    me = lax.axis_index(name)
    copies = []
    for k in range(1, n):
        other = lax.rem(me + k, n)
        part = ref if width is None else ref.at[pl.ds(pl.multiple_of(other * width, width), width)]
        copies.append(
            pltpu.make_async_remote_copy(
                src_ref=part,
                dst_ref=slots.at[k],
                send_sem=send.at[k],
                recv_sem=recv.at[k],
                device_id={name: other},
                device_id_type=MESH,
            )
        )
        copies[-1].start()
    return copies


def added(slots, name, n):
    me = lax.axis_index(name)
    acc = slots[me]
    for i in range(1, n):
        acc = acc + slots[lax.rem(me - i + n, n)]
    return acc


def finish_kernel(panel, offsets, axes, scale, damping, sens, prior, *rest):
    parts = rest[: len(offsets)]
    scene_rows, factor, info, spread_sens, out = rest[len(offsets) : len(offsets) + 5]
    mine, near, wide_slots, whole, written, s1, r1, s2, r2, s3, r3 = rest[len(offsets) + 5 :]
    barrier = pltpu.get_barrier_semaphore()
    for name, n in axes:
        me = lax.axis_index(name)
        for k in range(1, n):
            pl.semaphore_signal(
                barrier, inc=1, device_id={name: lax.rem(me + k, n)}, device_id_type=MESH
            )
    mine[...] = factor_scenes(panel, offsets, damping, sens, parts, out, info, spread_sens)
    rows = pltpu.make_async_copy(out, scene_rows, written)
    rows.start()
    pl.semaphore_wait(barrier, sum(n - 1 for _, n in axes))
    (tie, n), (scene, groups) = axes
    chunk = mine.shape[0] // n
    me = lax.axis_index(tie)
    own = pl.ds(pl.multiple_of(me * chunk, chunk), chunk)
    near[0] = mine[own]
    first = exchange(mine, near, s1, r1, tie, n, chunk)
    for copy in first:
        copy.wait_recv()
    wide_slots[0] = added(near, tie, n)
    second = exchange(wide_slots.at[0], wide_slots, s2, r2, scene, groups)
    for copy in second:
        copy.wait_recv()
    whole[own] = added(wide_slots, scene, groups)
    third = []
    for k in range(1, n):
        third.append(
            pltpu.make_async_remote_copy(
                src_ref=whole.at[own],
                dst_ref=whole.at[own],
                send_sem=s3.at[k],
                recv_sem=r3.at[k],
                device_id={tie: lax.rem(me + k, n)},
                device_id_type=MESH,
            )
        )
        third[-1].start()
    for copy in third:
        copy.wait_recv()
    shared = factor.shape[0]
    lane = lax.broadcasted_iota(jnp.int32, (shared, shared), 1)
    row = lax.broadcasted_iota(jnp.int32, (shared, shared), 0)
    value = jnp.concatenate([whole[:, :shared], whole[:, shared:]], 0)
    value = value * scale + jnp.where(lane == row, prior[...], 0.0)
    factor[...] = jnp.concatenate(eliminate([value], 0)[0], 0)
    for copy in first + second + third:
        copy.wait_send()
    rows.wait()


def factor_scenes(panel, offsets, damping, sens, parts, out, info, spread_sens):
    own, width, _ = info.shape
    spline = out.shape[1]
    half = width // 2
    beyond = width - spline
    for q in range(own):
        wide = jnp.concatenate([sens[q], jnp.zeros((spline, beyond), BF16)], 1)
        spread_sens[q] = jnp.concatenate([wide, jnp.zeros((beyond, width), BF16)], 0)
    row_index = lax.broadcasted_iota(jnp.int32, (width, width), 0)
    lane = lax.broadcasted_iota(jnp.int32, (width, width), 1)
    on_diagonal = (row_index == lane) & (row_index < spline)
    across = lane[:half, :half] - row_index[:half, :half]
    for q in range(own):
        held = [
            (part, q - offset, part.shape[0] // width)
            for offset, part in zip(offsets, parts)
            if offset <= q < offset + part.shape[0] // width
        ]
        packed = sum(part[at * width : (at + 1) * width] for part, at, _ in held)
        diagonal = sum(part[size * width + at : size * width + at + 1] for part, at, size in held)
        side, both = packed[:half], packed[half:]
        upper = jnp.where(across > 0, both, 0.0)
        first = jnp.where(across >= 0, both, upper.T)
        lower = jnp.where(across < 0, both, 0.0)
        last = lower + jnp.where(across == 0, diagonal, lower.T)
        top = jnp.concatenate([first, side], 1)
        bottom = jnp.concatenate([side.T, last], 1)
        whole = jnp.concatenate([top, bottom], 0)
        s = spread_sens[q]
        mixed = whole + sum(
            jnp.dot(piece, s, preferred_element_type=F32) for piece in two_parts(whole)
        )
        result = mixed + sum(over_rows(s, piece) for piece in two_parts(mixed))
        info[q] = result + jnp.where(on_diagonal, damping[q], 0.0)
    for start in range(0, spline, panel):
        base = start // LANES * LANES
        panels = [info[q, start : start + panel, base:] for q in range(own)]
        rows = eliminate(panels, start - base)
        if base:
            out[:, start : start + panel, :base] = jnp.zeros((own, panel, base), F32)
        after = start + panel
        for q in range(own):
            block = jnp.concatenate(rows[q], 0)
            out[q, start : start + panel, base:] = block
            high, low = two_parts(block)
            left = jnp.concatenate([high, high, low], 0)
            right = jnp.concatenate([high, low, high], 0)
            for top in range(after // LANES * LANES, width, LANES):
                skip = max(after - top, 0)
                update = over_rows(left[:, top - base : top - base + LANES], right[:, top - base :])
                info[q, top + skip : top + LANES, top:] -= update[skip:]
    total = info[0, spline:, half:]
    for q in range(1, own):
        total = total + info[q, spline:, half:]
    total = total[:, spline - half :]
    middle = (width - spline) // 2
    return jnp.concatenate([total[:middle], total[middle:]], 1)


def finish(parts, sensitivity, damping, prior, width, axes):
    own = damping.shape[0]
    spline = sensitivity.shape[1]
    beyond = width - spline
    (_, n), (_, groups) = axes
    mine = lax.dynamic_slice_in_dim(sensitivity, lax.axis_index("tie") * own, own)
    offsets = [offset for offset, _ in parts]
    scale = 1.0 / (own * n * groups)
    block = (beyond // 2 // n, 2 * beyond)
    dma = pltpu.SemaphoreType.DMA
    return pl.pallas_call(
        functools.partial(finish_kernel, PANEL, offsets, axes, scale),
        in_specs=[pl.BlockSpec(memory_space=pltpu.SMEM)] + [VMEM] * (2 + len(parts)),
        out_specs=[pl.BlockSpec(memory_space=pl.ANY), VMEM],
        scratch_shapes=[
            pltpu.VMEM((own, width, width), F32),
            pltpu.VMEM((own, width, width), BF16),
            pltpu.VMEM((own, spline, width), F32),
            pltpu.VMEM((beyond // 2, 2 * beyond), F32),
            pltpu.VMEM((n,) + block, F32),
            pltpu.VMEM((groups,) + block, F32),
            pltpu.VMEM((beyond // 2, 2 * beyond), F32),
            dma,
            dma((n,)),
            dma((n,)),
            dma((groups,)),
            dma((groups,)),
            dma((n,)),
            dma((n,)),
        ],
        out_shape=[
            jax.ShapeDtypeStruct((own, spline, width), F32),
            jax.ShapeDtypeStruct((beyond, beyond), F32),
        ],
        compiler_params=pltpu.CompilerParams(
            collective_id=0, has_side_effects=True, vmem_limit_bytes=32 << 20
        ),
        name="finish",
    )(damping, mine, prior[None, :], *(part for _, part in parts))


def emit_kernel(rows, factor, rows_out, factor_out, sems):
    copies = [
        pltpu.make_async_copy(rows, rows_out, sems.at[0]),
        pltpu.make_async_copy(factor, factor_out, sems.at[1]),
    ]
    for copy in copies:
        copy.start()
    for copy in copies:
        copy.wait()


def emit(scene_rows, factor):
    anywhere = pl.BlockSpec(memory_space=pl.ANY)
    return pl.pallas_call(
        emit_kernel,
        in_specs=[anywhere] * 2,
        out_specs=[anywhere] * 2,
        scratch_shapes=[pltpu.SemaphoreType.DMA((2,))],
        out_shape=[jax.ShapeDtypeStruct(x.shape, x.dtype) for x in (scene_rows, factor)],
        compiler_params=pltpu.CompilerParams(vmem_limit_bytes=1 << 20),
        name="emit",
    )(scene_rows, factor)


def on_device(axes, tie_rows, point_counts, pattern, sensitivity, damping, prior):
    sizes = dict(axes)
    own = damping.shape[0]
    width = tie_rows.shape[2]
    parts = merged_sums(tie_rows, point_counts, pattern, own, sizes["tie"])
    return emit(*finish(parts, sensitivity, damping, prior, width, axes))


def solution(mesh):
    axes = (("tie", mesh.shape["tie"]), ("scene", mesh.shape["scene"]))
    placed = (
        P("tie", None, None),
        P("tie"),
        P("scene", "tie"),
        P("scene", None, None),
        P(("scene", "tie")),
        P(),
    )
    return jax.shard_map(
        functools.partial(on_device, axes),
        mesh=mesh,
        in_specs=placed,
        out_specs=(P(("scene", "tie"), None, None), P()),
        check_vma=False,
    )
```

profile of v0, /device:TPU:0, one launch (start us, length us, event | category | flops | bytes accessed | tf_op | source)
XLA Modules:
  0.0 60.2 jit_solution(9561883897120751956)
XLA Ops:
  0.6 0.0 copy-start
  0.6 4.3 %shard_map.77 = (f32[520,128]{1,0:T(8,128)S(1)}, f32[520,128]{1,0:T(8,128)S(1)}) custom-call(s32[96]{0:T(128)} %counts.3, s32[16,96]{1,0:T(8,128)} %pattern.5, bf16[96,256,256]{2,1,0:T(8,128)(2,1)} %rows.5), custom_call_target="tpu_custom_call" | custom-call | tf_op jit(solution)/shard_map/pallas_call | solution.py:119
  5.0 1.1 %collective-permute-start = (f32[520,128]{1,0:T(8,128)S(1)}, f32[520,128]{1,0:T(8,128)S(1)}, u32[]{:S(2)}, u32[]{:S(2)}) collective-permute-start(f32[520,128]{1,0:T(8,128)S(1)} %get-tuple-element.15), channel_id=1, source_target_pairs={{0,1},{1,0},{2,3},{3,2},{4,5},{5,4},{6,7},{7,6},{8,9},{9,8},{10,11... | collective-permute-start | bytes 798728 | tf_op jit(solution)/shard_map/ppermute | solution.py:152
  6.1 1.2 %collective-permute-done.y = f32[520,128]{1,0:T(8,128)S(1)} collective-permute-done((f32[520,128]{1,0:T(8,128)S(1)}, f32[520,128]{1,0:T(8,128)S(1)}, u32[]{:S(2)}, u32[]{:S(2)}) %collective-permute-start) | collective-permute-done | bytes 266272 | tf_op jit(solution)/shard_map/ppermute | solution.py:152
  7.3 4.3 %shard_map.78 = (f32[520,128]{1,0:T(8,128)S(1)}, f32[520,128]{1,0:T(8,128)S(1)}) custom-call(s32[96]{0:T(128)} %counts.3, s32[16,96]{1,0:T(8,128)} %pattern.5, bf16[96,256,256]{2,1,0:T(8,128)(2,1)} %rows.5), custom_call_target="tpu_custom_call" | custom-call | tf_op jit(solution)/shard_map/pallas_call | solution.py:119
  11.6 0.9 %collective-permute-start.1 = (f32[520,128]{1,0:T(8,128)S(1)}, f32[520,128]{1,0:T(8,128)S(1)}, u32[]{:S(2)}, u32[]{:S(2)}) collective-permute-start(f32[520,128]{1,0:T(8,128)S(1)} %get-tuple-element.18), channel_id=1, source_target_pairs={{0,1},{1,0},{2,3},{3,2},{4,5},{5,4},{6,7},{7,6},{8,9},{9,8},{10,11... | collective-permute-start | bytes 798728 | tf_op jit(solution)/shard_map/ppermute | solution.py:152
  12.4 1.2 %collective-permute-done.1.y = f32[520,128]{1,0:T(8,128)S(1)} collective-permute-done((f32[520,128]{1,0:T(8,128)S(1)}, f32[520,128]{1,0:T(8,128)S(1)}, u32[]{:S(2)}, u32[]{:S(2)}) %collective-permute-start.1) | collective-permute-done | bytes 266272 | tf_op jit(solution)/shard_map/ppermute | solution.py:152
  13.6 0.7 %join.3 = f32[520,128]{1,0:T(8,128)} custom-call(f32[520,128]{1,0:T(8,128)S(1)} %get-tuple-element.17.x, f32[520,128]{1,0:T(8,128)S(1)} %collective-permute-done.1.y), custom_call_target="tpu_custom_call" | custom-call | tf_op jit(solution)/shard_map/join/pallas_call | solution.py:141
  14.3 0.0 copy-start.1
  14.3 0.0 copy-start.2
  14.3 7.1 %shard_map.79 = (f32[1032,128]{1,0:T(8,128)}, f32[1032,128]{1,0:T(8,128)S(1)}) custom-call(s32[96]{0:T(128)} %counts.3, s32[16,96]{1,0:T(8,128)} %pattern.5, bf16[96,256,256]{2,1,0:T(8,128)(2,1)} %rows.5), custom_call_target="tpu_custom_call" | custom-call | tf_op jit(solution)/shard_map/pallas_call | solution.py:119
  21.4 0.4 collective-permute-start.2
  21.9 2.3 %collective-permute-start.3 = (f32[520,128]{1,0:T(8,128)S(1)}, f32[520,128]{1,0:T(8,128)S(1)}, u32[]{:S(2)}, u32[]{:S(2)}) collective-permute-start(f32[520,128]{1,0:T(8,128)S(1)} %join.2), channel_id=1, source_target_pairs={{0,2},{1,3},{2,0},{3,1},{4,6},{5,7},{6,4},{7,5},{8,10},{9,11},{10,... | collective-permute-start | bytes 798728 | tf_op jit(solution)/shard_map/ppermute | solution.py:157
  24.2 0.1 collective-permute-start.4
  24.3 0.0 copy-done
  24.3 7.1 %collective-permute-done.3.rest_2_ = f32[520,128]{1,0:T(8,128)S(1)} collective-permute-done((f32[520,128]{1,0:T(8,128)S(1)}, f32[520,128]{1,0:T(8,128)S(1)}, u32[]{:S(2)}, u32[]{:S(2)}) %collective-permute-start.3) | collective-permute-done | bytes 266272 | tf_op jit(solution)/shard_map/ppermute | solution.py:157
  31.4 5.4 %collective-permute-done.4.rest_3_ = f32[520,128]{1,0:T(8,128)S(1)} collective-permute-done((f32[520,128]{1,0:T(8,128)}, f32[520,128]{1,0:T(8,128)S(1)}, u32[]{:S(2)}, u32[]{:S(2)}) %collective-permute-start.4) | collective-permute-done | bytes 266272 | tf_op jit(solution)/shard_map/ppermute | solution.py:157
  36.9 0.0 collective-permute-done.2.rest_1_
  36.9 0.0 copy-done.1
  36.9 0.0 copy-done.2
  36.9 22.3 %finish.1 = (f32[4,192,256]{2,1,0:T(8,128)S(1)}, f32[64,64]{1,0:T(8,128)S(1)}) custom-call(f32[4]{0:T(128)S(1)} %copy-done.1, bf16[4,192,192]{2,1,0:T(8,128)(2,1)S(1)} %constant_dynamic-slice_fusion.sens, f32[1,64]{1,0:T(1,128)S(1)} %bitcast.1, f32[1032,128]{1,0:T(8,128)S(1)} %get-tuple-element.20.rest_0_, f32[1032,128]{1,0:T(8,128)S(1)} %collective-permute-done.2.rest_1_, ...), custom_call_target="tpu_custom_call" | custom-call | tf_op jit(solution)/shard_map/finish/pallas_call | solution.py:374
  59.2 0.9 %emit.1 = (f32[4,192,256]{2,1,0:T(8,128)}, f32[64,64]{1,0:T(8,128)}) custom-call(f32[4,192,256]{2,1,0:T(8,128)S(1)} %get-tuple-element.24.rows, f32[64,64]{1,0:T(8,128)S(1)} %get-tuple-element.25.factor), custom_call_target="tpu_custom_call" | custom-call | tf_op jit(solution)/shard_map/emit/pallas_call | solution.py:418
  (2 shorter events, 0.1 us)
Async XLA Ops:
  0.6 23.7 %copy-start = (bf16[16,192,192]{2,1,0:T(8,128)(2,1)S(1)}, bf16[16,192,192]{2,1,0:T(8,128)(2,1)}, u32[]{:S(2)}) copy-start(bf16[16,192,192]{2,1,0:T(8,128)(2,1)} %param.9) | copy-start | bytes 3538948
  5.0 2.3 %collective-permute-start = (f32[520,128]{1,0:T(8,128)S(1)}, f32[520,128]{1,0:T(8,128)S(1)}, u32[]{:S(2)}, u32[]{:S(2)}) collective-permute-start(f32[520,128]{1,0:T(8,128)S(1)} %get-tuple-element.15), channel_id=1, source_target_pairs={{0,1},{1,0},{2,3},{3,2},{4,5},{5,4},{6,7},{7,6},{8,9},{9,8},{10,11... | collective-permute-start | bytes 798728 | tf_op jit(solution)/shard_map/ppermute | solution.py:152
  11.6 2.0 %collective-permute-start.1 = (f32[520,128]{1,0:T(8,128)S(1)}, f32[520,128]{1,0:T(8,128)S(1)}, u32[]{:S(2)}, u32[]{:S(2)}) collective-permute-start(f32[520,128]{1,0:T(8,128)S(1)} %get-tuple-element.18), channel_id=1, source_target_pairs={{0,1},{1,0},{2,3},{3,2},{4,5},{5,4},{6,7},{7,6},{8,9},{9,8},{10,11... | collective-permute-start | bytes 798728 | tf_op jit(solution)/shard_map/ppermute | solution.py:152
  14.3 22.6 %copy-start.1 = (f32[4]{0:T(128)S(1)}, f32[4]{0:T(128)}, u32[]{:S(2)}) copy-start(f32[4]{0:T(128)} %damping.1) | copy-start | bytes 52
  14.3 22.6 %copy-start.2 = (f32[64]{0:T(128)S(1)}, f32[64]{0:T(128)}, u32[]{:S(2)}) copy-start(f32[64]{0:T(128)} %param.11) | copy-start | bytes 772
  21.4 15.5 %collective-permute-start.2 = (f32[1032,128]{1,0:T(8,128)}, f32[1032,128]{1,0:T(8,128)S(1)}, u32[]{:S(2)}, u32[]{:S(2)}) collective-permute-start(f32[1032,128]{1,0:T(8,128)} %get-tuple-element.21), channel_id=1, source_target_pairs={{0,1},{1,0},{2,3},{3,2},{4,5},{5,4},{6,7},{7,6},{8,9},{9,8},{10,11... | collective-permute-start | bytes 1585160 | tf_op jit(solution)/shard_map/ppermute | solution.py:152
  21.9 9.6 %collective-permute-start.3 = (f32[520,128]{1,0:T(8,128)S(1)}, f32[520,128]{1,0:T(8,128)S(1)}, u32[]{:S(2)}, u32[]{:S(2)}) collective-permute-start(f32[520,128]{1,0:T(8,128)S(1)} %join.2), channel_id=1, source_target_pairs={{0,2},{1,3},{2,0},{3,1},{4,6},{5,7},{6,4},{7,5},{8,10},{9,11},{10,... | collective-permute-start | bytes 798728 | tf_op jit(solution)/shard_map/ppermute | solution.py:157
  24.2 12.7 %collective-permute-start.4 = (f32[520,128]{1,0:T(8,128)}, f32[520,128]{1,0:T(8,128)S(1)}, u32[]{:S(2)}, u32[]{:S(2)}) collective-permute-start(f32[520,128]{1,0:T(8,128)} %join.3), channel_id=1, source_target_pairs={{0,2},{1,3},{2,0},{3,1},{4,6},{5,7},{6,4},{7,5},{8,10},{9,11},{10,... | collective-permute-start | bytes 798728 | tf_op jit(solution)/shard_map/ppermute | solution.py:157
where the time goes:
time: 60.6 us; the launch traced here: 60.2 us
  Pallas kernels  39.6 us (65%)
  waiting for transfers between devices  14.9 us (25%)
  starting transfers between devices  4.83 us (8%)
  between operations  0.85 us (1%)
    pallas_call x1, Pallas kernels, finish(): pl.pallas_call(functools.partial(finish_kernel, PANEL, offsets, axes, sca...  22.3 us
    pallas_call x3, Pallas kernels, gram_sums(): pl.pallas_call(functools.partial(gram_kernel, groups, own, n // 2), in_sp...  15.7 us
    ppermute x2, waiting for transfers between devices, send_over(): lax.ppermute(x, 'tie', [(t, (t // 2 + hop) % pairs * 2 + t % 2) for t in...  12.6 us
    ppermute x2, starting transfers between devices, send_over(): lax.ppermute(x, 'tie', [(t, (t // 2 + hop) % pairs * 2 + t % 2) for t in...  2.42 us
    ppermute x3, starting transfers between devices, swap_cores(): return lax.ppermute(x, 'tie', [(t, t ^ 1) for t in range(n)])  2.4 us
    ppermute x3, waiting for transfers between devices, swap_cores(): return lax.ppermute(x, 'tie', [(t, t ^ 1) for t in range(n)])  2.34 us
  transfers between devices with their start and end apart: 5, of which 4 were waited for; matrix products, arithmetic and copies ran while one was open for 0% of the time, Pallas kernels for 0%

commit v1 on v0

--- a/solution.py
+++ b/solution.py
@@ -163,15 +163,22 @@
     tie_rows, point_counts, pattern = (
         pltpu.with_memory_space_constraint(x, pltpu.HBM) for x in (tie_rows, point_counts, pattern)
     )
-    for hop in range(1, n // 2):
-        for offset in range(0, own, size):
-            groups = [(hop, side, offset, size) for side in (1, 0)]
-            theirs, mine = gram_sums(tie_rows, point_counts, pattern, groups, own, n)
-            both = join(mine, swap_cores(theirs, n))
-            both, point_counts = lax.optimization_barrier((both, point_counts))
-            parts.append((offset, send_over(both, n, hop)))
-    groups = [(0, 1, 0, own), (0, 0, 0, own)]
-    theirs, mine = gram_sums(tie_rows, point_counts, pattern, groups, own, n)
+    sends = [(hop, offset) for hop in range(1, n // 2) for offset in range(0, own, size)]
+    near = [(0, 1, 0, own)]
+    for k, (hop, offset) in enumerate(sends):
+        groups = [(hop, side, offset, size) for side in (1, 0)]
+        if k == len(sends) - 1:
+            groups += near
+        sums = gram_sums(tie_rows, point_counts, pattern, groups, own, n)
+        both = join(sums[1], swap_cores(sums[0], n))
+        both, point_counts = lax.optimization_barrier((both, point_counts))
+        parts.append((offset, send_over(both, n, hop)))
+    if sends:
+        theirs = sums[2]
+        (mine,) = gram_sums(tie_rows, point_counts, pattern, [(0, 0, 0, own)], own, n)
+    else:
+        groups = near + [(0, 0, 0, own)]
+        theirs, mine = gram_sums(tie_rows, point_counts, pattern, groups, own, n)
     return [(0, mine), (0, swap_cores(theirs, n))] + parts
 
 
@@ -396,7 +403,7 @@
             jax.ShapeDtypeStruct((beyond, beyond), F32),
         ],
         compiler_params=pltpu.CompilerParams(
-            collective_id=0, has_side_effects=True, vmem_limit_bytes=32 << 20
+            collective_id=0, has_side_effects=True, vmem_limit_bytes=12 << 20
         ),
         name="finish",
     )(damping, mine, prior[None, :], *(part for _, part in parts))

time: 60.6 us -> 53.3 us (0.88)
  waiting for transfers between devices: 14.9 us -> 7.92 us
  Pallas kernels: 39.6 us -> 38.5 us
  starting transfers between devices: 4.83 us -> 5.63 us
    ppermute x2, waiting for transfers between devices: 12.6 us -> 6.75 us  [send_over(): lax.ppermute(x, 'tie', [(t, (t // 2 + hop) % pairs * 2 + t % 2) for t in...]
    ppermute x3, waiting for transfers between devices: 2.34 us -> 1.17 us  [swap_cores(): return lax.ppermute(x, 'tie', [(t, t ^ 1) for t in range(n)])]
    ppermute x2, starting transfers between devices: 2.42 us -> 3.47 us  [send_over(): lax.ppermute(x, 'tie', [(t, (t // 2 + hop) % pairs * 2 + t % 2) for t in...]
    pallas_call x2, Pallas kernels: 0.76 us -> 0.06 us  [join(): pl.pallas_call(join_kernel, in_specs=[VMEM] * 2, out_specs=VMEM, out_shap...]
  transfers between devices with their start and end apart: 5 -> 5, of which waited for: 4 -> 3; matrix products, arithmetic and copies ran while one was open for 0% -> 0% of each run, Pallas kernels for 0% -> 8%
where the time goes in v1:
time: 53.3 us; the launch traced here: 52.9 us
  Pallas kernels  38.5 us (72%)
  waiting for transfers between devices  7.92 us (15%)
  starting transfers between devices  5.63 us (11%)
  between operations  0.86 us (2%)
    pallas_call x1, Pallas kernels, finish(): pl.pallas_call(functools.partial(finish_kernel, PANEL, offsets, axes, sca...  22 us
    pallas_call x3, Pallas kernels, gram_sums(): pl.pallas_call(functools.partial(gram_kernel, groups, own, n // 2), in_sp...  15.5 us
    ppermute x2, waiting for transfers between devices, send_over(): lax.ppermute(x, 'tie', [(t, (t // 2 + hop) % pairs * 2 + t % 2) for t in...  6.75 us
    ppermute x2, starting transfers between devices, send_over(): lax.ppermute(x, 'tie', [(t, (t // 2 + hop) % pairs * 2 + t % 2) for t in...  3.47 us
    ppermute x3, starting transfers between devices, swap_cores(): return lax.ppermute(x, 'tie', [(t, t ^ 1) for t in range(n)])  2.16 us
    ppermute x3, waiting for transfers between devices, swap_cores(): return lax.ppermute(x, 'tie', [(t, t ^ 1) for t in range(n)])  1.17 us
  transfers between devices with their start and end apart: 5, of which 3 were waited for; matrix products, arithmetic and copies ran while one was open for 0% of the time, Pallas kernels for 8%

profile of v1, /device:TPU:0, one launch (start us, length us, event | category | flops | bytes accessed | tf_op | source)
XLA Modules:
  0.0 52.9 jit_solution(11658317454749919058)
XLA Ops:
  0.6 0.0 copy-start
  0.6 4.3 %shard_map.77 = (f32[520,128]{1,0:T(8,128)S(1)}, f32[520,128]{1,0:T(8,128)S(1)}) custom-call(s32[96]{0:T(128)} %counts.3, s32[16,96]{1,0:T(8,128)} %pattern.5, bf16[96,256,256]{2,1,0:T(8,128)(2,1)} %rows.5), custom_call_target="tpu_custom_call" | custom-call | tf_op jit(solution)/shard_map/pallas_call | solution.py:119
  5.0 1.1 %collective-permute-start = (f32[520,128]{1,0:T(8,128)S(1)}, f32[520,128]{1,0:T(8,128)S(1)}, u32[]{:S(2)}, u32[]{:S(2)}) collective-permute-start(f32[520,128]{1,0:T(8,128)S(1)} %get-tuple-element.14), channel_id=1, source_target_pairs={{0,1},{1,0},{2,3},{3,2},{4,5},{5,4},{6,7},{7,6},{8,9},{9,8},{10,11... | collective-permute-start | bytes 798728 | tf_op jit(solution)/shard_map/ppermute | solution.py:152
  6.1 1.2 %collective-permute-done.y = f32[520,128]{1,0:T(8,128)S(1)} collective-permute-done((f32[520,128]{1,0:T(8,128)S(1)}, f32[520,128]{1,0:T(8,128)S(1)}, u32[]{:S(2)}, u32[]{:S(2)}) %collective-permute-start) | collective-permute-done | bytes 266272 | tf_op jit(solution)/shard_map/ppermute | solution.py:152
  7.3 6.8 %shard_map.78 = (f32[520,128]{1,0:T(8,128)S(1)}, f32[520,128]{1,0:T(8,128)S(1)}, f32[1032,128]{1,0:T(8,128)}) custom-call(s32[96]{0:T(128)} %counts.3, s32[16,96]{1,0:T(8,128)} %pattern.5, bf16[96,256,256]{2,1,0:T(8,128)(2,1)} %rows.5), custom_call_target="tpu_custom_call" | custom-call | tf_op jit(solution)/shard_map/pallas_call | solution.py:119
  14.1 1.0 %collective-permute-start.1 = (f32[520,128]{1,0:T(8,128)S(1)}, f32[520,128]{1,0:T(8,128)S(1)}, u32[]{:S(2)}, u32[]{:S(2)}) collective-permute-start(f32[520,128]{1,0:T(8,128)S(1)} %get-tuple-element.17), channel_id=1, source_target_pairs={{0,1},{1,0},{2,3},{3,2},{4,5},{5,4},{6,7},{7,6},{8,9},{9,8},{10,11... | collective-permute-start | bytes 798728 | tf_op jit(solution)/shard_map/ppermute | solution.py:152
  15.0 0.1 collective-permute-start.2
  15.1 2.4 %collective-permute-start.3 = (f32[520,128]{1,0:T(8,128)S(1)}, f32[520,128]{1,0:T(8,128)S(1)}, u32[]{:S(2)}, u32[]{:S(2)}) collective-permute-start(f32[520,128]{1,0:T(8,128)S(1)} %join.2), channel_id=1, source_target_pairs={{0,2},{1,3},{2,0},{3,1},{4,6},{5,7},{6,4},{7,5},{8,10},{9,11},{10,... | collective-permute-start | bytes 798728 | tf_op jit(solution)/shard_map/ppermute | solution.py:157
  17.5 0.0 collective-permute-done.1.y
  17.5 1.1 %collective-permute-start.4 = (f32[520,128]{1,0:T(8,128)S(1)}, f32[520,128]{1,0:T(8,128)S(1)}, u32[]{:S(2)}, u32[]{:S(2)}) collective-permute-start(f32[520,128]{1,0:T(8,128)S(1)} %join.3), channel_id=1, source_target_pairs={{0,2},{1,3},{2,0},{3,1},{4,6},{5,7},{6,4},{7,5},{8,10},{9,11},{10,... | collective-permute-start | bytes 798728 | tf_op jit(solution)/shard_map/ppermute | solution.py:157
  18.6 0.0 copy-done
  18.6 0.0 copy-start.1
  18.7 0.0 copy-start.2
  18.7 4.5 %shard_map.79.rest_0_ = f32[1032,128]{1,0:T(8,128)S(1)} custom-call(s32[96]{0:T(128)} %counts.3, s32[16,96]{1,0:T(8,128)} %pattern.5, bf16[96,256,256]{2,1,0:T(8,128)(2,1)} %rows.5), custom_call_target="tpu_custom_call" | custom-call | tf_op jit(solution)/shard_map/pallas_call | solution.py:119
  23.1 1.6 %collective-permute-done.3.rest_2_ = f32[520,128]{1,0:T(8,128)S(1)} collective-permute-done((f32[520,128]{1,0:T(8,128)S(1)}, f32[520,128]{1,0:T(8,128)S(1)}, u32[]{:S(2)}, u32[]{:S(2)}) %collective-permute-start.3) | collective-permute-done | bytes 266272 | tf_op jit(solution)/shard_map/ppermute | solution.py:157
  24.7 0.0 collective-permute-done.2.rest_1_
  24.7 5.2 %collective-permute-done.4.rest_3_ = f32[520,128]{1,0:T(8,128)S(1)} collective-permute-done((f32[520,128]{1,0:T(8,128)S(1)}, f32[520,128]{1,0:T(8,128)S(1)}, u32[]{:S(2)}, u32[]{:S(2)}) %collective-permute-start.4) | collective-permute-done | bytes 266272 | tf_op jit(solution)/shard_map/ppermute | solution.py:157
  29.9 0.0 copy-done.1
  29.9 0.0 copy-done.2
  29.9 22.0 %finish.1 = (f32[4,192,256]{2,1,0:T(8,128)S(1)}, f32[64,64]{1,0:T(8,128)S(1)}) custom-call(f32[4]{0:T(128)S(1)} %copy-done.1, bf16[4,192,192]{2,1,0:T(8,128)(2,1)S(1)} %constant_dynamic-slice_fusion.sens, f32[1,64]{1,0:T(1,128)S(1)} %bitcast.1, f32[1032,128]{1,0:T(8,128)S(1)} %shard_map.79.rest_0_, f32[1032,128]{1,0:T(8,128)S(1)} %collective-permute-done.2.rest_1_, ...), custom_call_target="tpu_custom_call" | custom-call | tf_op jit(solution)/shard_map/finish/pallas_call | solution.py:381
  51.9 0.9 %emit.1 = (f32[4,192,256]{2,1,0:T(8,128)}, f32[64,64]{1,0:T(8,128)}) custom-call(f32[4,192,256]{2,1,0:T(8,128)S(1)} %get-tuple-element.22.rows, f32[64,64]{1,0:T(8,128)S(1)} %get-tuple-element.23.factor), custom_call_target="tpu_custom_call" | custom-call | tf_op jit(solution)/shard_map/emit/pallas_call | solution.py:425
  (3 shorter events, 0.1 us)
Async XLA Ops:
  0.6 18.0 %copy-start = (bf16[16,192,192]{2,1,0:T(8,128)(2,1)S(1)}, bf16[16,192,192]{2,1,0:T(8,128)(2,1)}, u32[]{:S(2)}) copy-start(bf16[16,192,192]{2,1,0:T(8,128)(2,1)} %param.9) | copy-start | bytes 3538948
  5.0 2.3 %collective-permute-start = (f32[520,128]{1,0:T(8,128)S(1)}, f32[520,128]{1,0:T(8,128)S(1)}, u32[]{:S(2)}, u32[]{:S(2)}) collective-permute-start(f32[520,128]{1,0:T(8,128)S(1)} %get-tuple-element.14), channel_id=1, source_target_pairs={{0,1},{1,0},{2,3},{3,2},{4,5},{5,4},{6,7},{7,6},{8,9},{9,8},{10,11... | collective-permute-start | bytes 798728 | tf_op jit(solution)/shard_map/ppermute | solution.py:152
  14.1 3.4 %collective-permute-start.1 = (f32[520,128]{1,0:T(8,128)S(1)}, f32[520,128]{1,0:T(8,128)S(1)}, u32[]{:S(2)}, u32[]{:S(2)}) collective-permute-start(f32[520,128]{1,0:T(8,128)S(1)} %get-tuple-element.17), channel_id=1, source_target_pairs={{0,1},{1,0},{2,3},{3,2},{4,5},{5,4},{6,7},{7,6},{8,9},{9,8},{10,11... | collective-permute-start | bytes 798728 | tf_op jit(solution)/shard_map/ppermute | solution.py:152
  15.0 9.7 %collective-permute-start.2 = (f32[1032,128]{1,0:T(8,128)}, f32[1032,128]{1,0:T(8,128)S(1)}, u32[]{:S(2)}, u32[]{:S(2)}) collective-permute-start(f32[1032,128]{1,0:T(8,128)} %get-tuple-element.19), channel_id=1, source_target_pairs={{0,1},{1,0},{2,3},{3,2},{4,5},{5,4},{6,7},{7,6},{8,9},{9,8},{10,11... | collective-permute-start | bytes 1585160 | tf_op jit(solution)/shard_map/ppermute | solution.py:152
  15.1 9.6 %collective-permute-start.3 = (f32[520,128]{1,0:T(8,128)S(1)}, f32[520,128]{1,0:T(8,128)S(1)}, u32[]{:S(2)}, u32[]{:S(2)}) collective-permute-start(f32[520,128]{1,0:T(8,128)S(1)} %join.2), channel_id=1, source_target_pairs={{0,2},{1,3},{2,0},{3,1},{4,6},{5,7},{6,4},{7,5},{8,10},{9,11},{10,... | collective-permute-start | bytes 798728 | tf_op jit(solution)/shard_map/ppermute | solution.py:157
  17.5 12.4 %collective-permute-start.4 = (f32[520,128]{1,0:T(8,128)S(1)}, f32[520,128]{1,0:T(8,128)S(1)}, u32[]{:S(2)}, u32[]{:S(2)}) collective-permute-start(f32[520,128]{1,0:T(8,128)S(1)} %join.3), channel_id=1, source_target_pairs={{0,2},{1,3},{2,0},{3,1},{4,6},{5,7},{6,4},{7,5},{8,10},{9,11},{10,... | collective-permute-start | bytes 798728 | tf_op jit(solution)/shard_map/ppermute | solution.py:157
  18.6 11.2 %copy-start.1 = (f32[4]{0:T(128)S(1)}, f32[4]{0:T(128)}, u32[]{:S(2)}) copy-start(f32[4]{0:T(128)} %damping.1) | copy-start | bytes 52
  18.7 11.2 %copy-start.2 = (f32[64]{0:T(128)S(1)}, f32[64]{0:T(128)}, u32[]{:S(2)}) copy-start(f32[64]{0:T(128)} %param.11) | copy-start | bytes 772

commit v2 on v0

--- a/solution.py
+++ b/solution.py
@@ -163,16 +163,19 @@
     tie_rows, point_counts, pattern = (
         pltpu.with_memory_space_constraint(x, pltpu.HBM) for x in (tie_rows, point_counts, pattern)
     )
+    offsets = range(0, own, size)
     for hop in range(1, n // 2):
-        for offset in range(0, own, size):
-            groups = [(hop, side, offset, size) for side in (1, 0)]
-            theirs, mine = gram_sums(tie_rows, point_counts, pattern, groups, own, n)
-            both = join(mine, swap_cores(theirs, n))
+        groups = [(hop, side, offset, size) for side in (1, 0) for offset in offsets]
+        sums = gram_sums(tie_rows, point_counts, pattern, groups, own, n)
+        swapped = [swap_cores(theirs, n) for theirs in sums[: len(offsets)]]
+        for offset, mine, theirs in zip(offsets, sums[len(offsets) :], swapped):
+            both = join(mine, theirs)
             both, point_counts = lax.optimization_barrier((both, point_counts))
             parts.append((offset, send_over(both, n, hop)))
-    groups = [(0, 1, 0, own), (0, 0, 0, own)]
-    theirs, mine = gram_sums(tie_rows, point_counts, pattern, groups, own, n)
-    return [(0, mine), (0, swap_cores(theirs, n))] + parts
+    groups = [(0, 1, offset, size) for offset in offsets] + [(0, 0, 0, own)]
+    sums = gram_sums(tie_rows, point_counts, pattern, groups, own, n)
+    swapped = [(o, swap_cores(theirs, n)) for o, theirs in zip(offsets, sums)]
+    return [(0, sums[-1])] + swapped + parts
 
 
 def two_parts(x):
@@ -396,7 +399,7 @@
             jax.ShapeDtypeStruct((beyond, beyond), F32),
         ],
         compiler_params=pltpu.CompilerParams(
-            collective_id=0, has_side_effects=True, vmem_limit_bytes=32 << 20
+            collective_id=0, has_side_effects=True, vmem_limit_bytes=12 << 20
         ),
         name="finish",
     )(damping, mine, prior[None, :], *(part for _, part in parts))

time: 60.6 us -> 48.8 us (0.81)
  waiting for transfers between devices: 14.9 us -> 6.89 us
  Pallas kernels: 39.6 us -> 35.8 us
    ppermute x2, waiting for transfers between devices: 12.6 us -> 5.46 us  [send_over(): lax.ppermute(x, 'tie', [(t, (t // 2 + hop) % pairs * 2 + t % 2) for t in...]
    pallas_call x3 -> x2, Pallas kernels: 15.7 us -> 12.3 us  [gram_sums(): pl.pallas_call(functools.partial(gram_kernel, groups, own, n // 2), in_sp...]
    ppermute x3 -> x4, waiting for transfers between devices: 2.34 us -> 1.43 us  [swap_cores(): return lax.ppermute(x, 'tie', [(t, t ^ 1) for t in range(n)])]
    ppermute x3 -> x4, starting transfers between devices: 2.4 us -> 2.26 us  [swap_cores(): return lax.ppermute(x, 'tie', [(t, t ^ 1) for t in range(n)])]
  transfers between devices with their start and end apart: 5 -> 6, of which waited for: 4 -> 4; matrix products, arithmetic and copies ran while one was open for 0% -> 0% of each run, Pallas kernels for 0% -> 14%
where the time goes in v2:
time: 48.8 us; the launch traced here: 48.6 us
  Pallas kernels  35.8 us (73%)
  waiting for transfers between devices  6.89 us (14%)
  starting transfers between devices  5.16 us (11%)
  between operations  0.69 us (1%)
    pallas_call x1, Pallas kernels, finish(): pl.pallas_call(functools.partial(finish_kernel, PANEL, offsets, axes, sca...  21.8 us
    pallas_call x2, Pallas kernels, gram_sums(): pl.pallas_call(functools.partial(gram_kernel, groups, own, n // 2), in_sp...  12.3 us
    ppermute x2, waiting for transfers between devices, send_over(): lax.ppermute(x, 'tie', [(t, (t // 2 + hop) % pairs * 2 + t % 2) for t in...  5.46 us
    ppermute x2, starting transfers between devices, send_over(): lax.ppermute(x, 'tie', [(t, (t // 2 + hop) % pairs * 2 + t % 2) for t in...  2.9 us
    ppermute x4, starting transfers between devices, swap_cores(): return lax.ppermute(x, 'tie', [(t, t ^ 1) for t in range(n)])  2.26 us
    ppermute x4, waiting for transfers between devices, swap_cores(): return lax.ppermute(x, 'tie', [(t, t ^ 1) for t in range(n)])  1.43 us
  transfers between devices with their start and end apart: 6, of which 4 were waited for; matrix products, arithmetic and copies ran while one was open for 0% of the time, Pallas kernels for 14%

profile of v2, /device:TPU:0, one launch (start us, length us, event | category | flops | bytes accessed | tf_op | source)
XLA Modules:
  0.0 48.6 jit_solution(16172803825245614645)
XLA Ops:
  0.6 0.0 copy-start
  0.6 5.6 %shard_map.77 = (f32[520,128]{1,0:T(8,128)S(1)}, f32[520,128]{1,0:T(8,128)S(1)}, f32[520,128]{1,0:T(8,128)S(1)}, f32[520,128]{1,0:T(8,128)S(1)}) custom-call(s32[96]{0:T(128)} %counts.2, s32[16,96]{1,0:T(8,128)} %pattern.3, bf16[96,256,256]{2,1,0:T(8,128)(2,1)} %rows.3), custom_call_target="tpu_custom_call" | custom-call | tf_op jit(solution)/shard_map/pallas_call | solution.py:119
  6.2 1.6 %collective-permute-start.1 = (f32[520,128]{1,0:T(8,128)S(1)}, f32[520,128]{1,0:T(8,128)S(1)}, u32[]{:S(2)}, u32[]{:S(2)}) collective-permute-start(f32[520,128]{1,0:T(8,128)S(1)} %get-tuple-element.18), channel_id=1, source_target_pairs={{0,1},{1,0},{2,3},{3,2},{4,5},{5,4},{6,7},{7,6},{8,9},{9,8},{10,11... | collective-permute-start | bytes 798728 | tf_op jit(solution)/shard_map/ppermute | solution.py:152
  7.9 0.1 collective-permute-start
  7.9 1.1 %collective-permute-done.1.y = f32[520,128]{1,0:T(8,128)S(1)} collective-permute-done((f32[520,128]{1,0:T(8,128)S(1)}, f32[520,128]{1,0:T(8,128)S(1)}, u32[]{:S(2)}, u32[]{:S(2)}) %collective-permute-start.1) | collective-permute-done | bytes 266272 | tf_op jit(solution)/shard_map/ppermute | solution.py:152
  9.1 0.3 collective-permute-done.y
  9.4 0.7 %join.2 = f32[520,128]{1,0:T(8,128)} custom-call(f32[520,128]{1,0:T(8,128)S(1)} %get-tuple-element.15.x, f32[520,128]{1,0:T(8,128)S(1)} %collective-permute-done.y), custom_call_target="tpu_custom_call" | custom-call | tf_op jit(solution)/shard_map/join/pallas_call | solution.py:141
  10.2 0.0 copy-start.1
  10.2 0.0 copy-start.2
  10.2 2.9 %collective-permute-start.5 = (f32[520,128]{1,0:T(8,128)}, f32[520,128]{1,0:T(8,128)S(1)}, u32[]{:S(2)}, u32[]{:S(2)}) collective-permute-start(f32[520,128]{1,0:T(8,128)} %join.2), channel_id=1, source_target_pairs={{0,2},{1,3},{2,0},{3,1},{4,6},{5,7},{6,4},{7,5},{8,10},{9,11},{10,... | collective-permute-start | bytes 798728 | tf_op jit(solution)/shard_map/ppermute | solution.py:157
  13.0 0.0 collective-permute-start.4
  13.1 6.7 %shard_map.78 = (f32[520,128]{1,0:T(8,128)}, f32[520,128]{1,0:T(8,128)}, f32[1032,128]{1,0:T(8,128)S(1)}) custom-call(s32[96]{0:T(128)} %counts.2, s32[16,96]{1,0:T(8,128)} %pattern.3, bf16[96,256,256]{2,1,0:T(8,128)(2,1)} %rows.3), custom_call_target="tpu_custom_call" | custom-call | tf_op jit(solution)/shard_map/pallas_call | solution.py:119
  19.8 0.1 collective-permute-start.2
  19.9 0.4 collective-permute-start.3
  20.4 0.0 copy-done
  20.4 0.1 collective-permute-done.5.rest_4_
  20.5 5.4 %collective-permute-done.4.rest_3_ = f32[520,128]{1,0:T(8,128)S(1)} collective-permute-done((f32[520,128]{1,0:T(8,128)S(1)}, f32[520,128]{1,0:T(8,128)S(1)}, u32[]{:S(2)}, u32[]{:S(2)}) %collective-permute-start.4) | collective-permute-done | bytes 266272 | tf_op jit(solution)/shard_map/ppermute | solution.py:157
  25.9 0.0 collective-permute-done.2.rest_1_
  25.9 0.0 collective-permute-done.3.rest_2_
  25.9 0.0 copy-done.1
  25.9 0.0 copy-done.2
  25.9 21.8 %finish.1 = (f32[4,192,256]{2,1,0:T(8,128)S(1)}, f32[64,64]{1,0:T(8,128)S(1)}) custom-call(f32[4]{0:T(128)S(1)} %copy-done.1, bf16[4,192,192]{2,1,0:T(8,128)(2,1)S(1)} %constant_dynamic-slice_fusion.sens, f32[1,64]{1,0:T(1,128)S(1)} %bitcast.1, f32[1032,128]{1,0:T(8,128)S(1)} %get-tuple-element.21.rest_0_, f32[520,128]{1,0:T(8,128)S(1)} %collective-permute-done.2.rest_1_, ...), custom_call_target="tpu_custom_call" | custom-call | tf_op jit(solution)/shard_map/finish/pallas_call | solution.py:377
  47.7 0.9 %emit.1 = (f32[4,192,256]{2,1,0:T(8,128)}, f32[64,64]{1,0:T(8,128)}) custom-call(f32[4,192,256]{2,1,0:T(8,128)S(1)} %get-tuple-element.26.rows, f32[64,64]{1,0:T(8,128)S(1)} %get-tuple-element.27.factor), custom_call_target="tpu_custom_call" | custom-call | tf_op jit(solution)/shard_map/emit/pallas_call | solution.py:421
  (2 shorter events, 0.1 us)
Async XLA Ops:
  0.6 19.7 %copy-start = (bf16[16,192,192]{2,1,0:T(8,128)(2,1)S(1)}, bf16[16,192,192]{2,1,0:T(8,128)(2,1)}, u32[]{:S(2)}) copy-start(bf16[16,192,192]{2,1,0:T(8,128)(2,1)} %param.9) | copy-start | bytes 3538948
  6.2 2.8 %collective-permute-start.1 = (f32[520,128]{1,0:T(8,128)S(1)}, f32[520,128]{1,0:T(8,128)S(1)}, u32[]{:S(2)}, u32[]{:S(2)}) collective-permute-start(f32[520,128]{1,0:T(8,128)S(1)} %get-tuple-element.18), channel_id=1, source_target_pairs={{0,1},{1,0},{2,3},{3,2},{4,5},{5,4},{6,7},{7,6},{8,9},{9,8},{10,11... | collective-permute-start | bytes 798728 | tf_op jit(solution)/shard_map/ppermute | solution.py:152
  7.9 1.5 %collective-permute-start = (f32[520,128]{1,0:T(8,128)S(1)}, f32[520,128]{1,0:T(8,128)S(1)}, u32[]{:S(2)}, u32[]{:S(2)}) collective-permute-start(f32[520,128]{1,0:T(8,128)S(1)} %get-tuple-element.16), channel_id=1, source_target_pairs={{0,1},{1,0},{2,3},{3,2},{4,5},{5,4},{6,7},{7,6},{8,9},{9,8},{10,11... | collective-permute-start | bytes 798728 | tf_op jit(solution)/shard_map/ppermute | solution.py:152
  10.2 15.7 %copy-start.1 = (f32[4]{0:T(128)S(1)}, f32[4]{0:T(128)}, u32[]{:S(2)}) copy-start(f32[4]{0:T(128)} %damping.1) | copy-start | bytes 52
  10.2 15.7 %copy-start.2 = (f32[64]{0:T(128)S(1)}, f32[64]{0:T(128)}, u32[]{:S(2)}) copy-start(f32[64]{0:T(128)} %param.11) | copy-start | bytes 772
  10.2 10.3 %collective-permute-start.5 = (f32[520,128]{1,0:T(8,128)}, f32[520,128]{1,0:T(8,128)S(1)}, u32[]{:S(2)}, u32[]{:S(2)}) collective-permute-start(f32[520,128]{1,0:T(8,128)} %join.2), channel_id=1, source_target_pairs={{0,2},{1,3},{2,0},{3,1},{4,6},{5,7},{6,4},{7,5},{8,10},{9,11},{10,... | collective-permute-start | bytes 798728 | tf_op jit(solution)/shard_map/ppermute | solution.py:157
  13.0 12.8 %collective-permute-start.4 = (f32[520,128]{1,0:T(8,128)S(1)}, f32[520,128]{1,0:T(8,128)S(1)}, u32[]{:S(2)}, u32[]{:S(2)}) collective-permute-start(f32[520,128]{1,0:T(8,128)S(1)} %join.3), channel_id=1, source_target_pairs={{0,2},{1,3},{2,0},{3,1},{4,6},{5,7},{6,4},{7,5},{8,10},{9,11},{10,... | collective-permute-start | bytes 798728 | tf_op jit(solution)/shard_map/ppermute | solution.py:157
  19.8 6.1 %collective-permute-start.2 = (f32[520,128]{1,0:T(8,128)}, f32[520,128]{1,0:T(8,128)S(1)}, u32[]{:S(2)}, u32[]{:S(2)}) collective-permute-start(f32[520,128]{1,0:T(8,128)} %get-tuple-element.22), channel_id=1, source_target_pairs={{0,1},{1,0},{2,3},{3,2},{4,5},{5,4},{6,7},{7,6},{8,9},{9,8},{10,11... | collective-permute-start | bytes 798728 | tf_op jit(solution)/shard_map/ppermute | solution.py:152
  19.9 5.9 %collective-permute-start.3 = (f32[520,128]{1,0:T(8,128)}, f32[520,128]{1,0:T(8,128)S(1)}, u32[]{:S(2)}, u32[]{:S(2)}) collective-permute-start(f32[520,128]{1,0:T(8,128)} %get-tuple-element.23), channel_id=1, source_target_pairs={{0,1},{1,0},{2,3},{3,2},{4,5},{5,4},{6,7},{7,6},{8,9},{9,8},{10,11... | collective-permute-start | bytes 798728 | tf_op jit(solution)/shard_map/ppermute | solution.py:152

commit v3 on v2

--- a/solution.py
+++ b/solution.py
@@ -406,10 +406,10 @@
 
 
 def emit_kernel(rows, factor, rows_out, factor_out, sems):
-    copies = [
-        pltpu.make_async_copy(rows, rows_out, sems.at[0]),
-        pltpu.make_async_copy(factor, factor_out, sems.at[1]),
-    ]
+    own = rows.shape[0]
+    copies = [pltpu.make_async_copy(factor, factor_out, sems.at[own])]
+    for q in range(own):
+        copies.append(pltpu.make_async_copy(rows.at[q], rows_out.at[q], sems.at[q]))
     for copy in copies:
         copy.start()
     for copy in copies:
@@ -422,7 +422,7 @@
         emit_kernel,
         in_specs=[anywhere] * 2,
         out_specs=[anywhere] * 2,
-        scratch_shapes=[pltpu.SemaphoreType.DMA((2,))],
+        scratch_shapes=[pltpu.SemaphoreType.DMA((scene_rows.shape[0] + 1,))],
         out_shape=[jax.ShapeDtypeStruct(x.shape, x.dtype) for x in (scene_rows, factor)],
         compiler_params=pltpu.CompilerParams(vmem_limit_bytes=1 << 20),
         name="emit",

time: 48.8 us -> 48.9 us (level)
  no operation moved by 1% of the time
where the time goes in v3:
time: 48.9 us; the launch traced here: 48.6 us
  Pallas kernels  35.8 us (73%)
  waiting for transfers between devices  6.89 us (14%)
  starting transfers between devices  5.16 us (11%)
  between operations  0.69 us (1%)
    pallas_call x1, Pallas kernels, finish(): pl.pallas_call(functools.partial(finish_kernel, PANEL, offsets, axes, sca...  21.8 us
    pallas_call x2, Pallas kernels, gram_sums(): pl.pallas_call(functools.partial(gram_kernel, groups, own, n // 2), in_sp...  12.3 us
    ppermute x2, waiting for transfers between devices, send_over(): lax.ppermute(x, 'tie', [(t, (t // 2 + hop) % pairs * 2 + t % 2) for t in...  5.46 us
    ppermute x2, starting transfers between devices, send_over(): lax.ppermute(x, 'tie', [(t, (t // 2 + hop) % pairs * 2 + t % 2) for t in...  2.9 us
    ppermute x4, starting transfers between devices, swap_cores(): return lax.ppermute(x, 'tie', [(t, t ^ 1) for t in range(n)])  2.26 us
    ppermute x4, waiting for transfers between devices, swap_cores(): return lax.ppermute(x, 'tie', [(t, t ^ 1) for t in range(n)])  1.43 us
  transfers between devices with their start and end apart: 6, of which 4 were waited for; matrix products, arithmetic and copies ran while one was open for 0% of the time, Pallas kernels for 14%

profile of v3, /device:TPU:0, one launch (start us, length us, event | category | flops | bytes accessed | tf_op | source)
XLA Modules:
  0.0 48.6 jit_solution(4918997753656706636)
XLA Ops:
  0.6 0.0 copy-start
  0.6 5.6 %shard_map.77 = (f32[520,128]{1,0:T(8,128)S(1)}, f32[520,128]{1,0:T(8,128)S(1)}, f32[520,128]{1,0:T(8,128)S(1)}, f32[520,128]{1,0:T(8,128)S(1)}) custom-call(s32[96]{0:T(128)} %counts.2, s32[16,96]{1,0:T(8,128)} %pattern.3, bf16[96,256,256]{2,1,0:T(8,128)(2,1)} %rows.3), custom_call_target="tpu_custom_call" | custom-call | tf_op jit(solution)/shard_map/pallas_call | solution.py:119
  6.2 1.6 %collective-permute-start.1 = (f32[520,128]{1,0:T(8,128)S(1)}, f32[520,128]{1,0:T(8,128)S(1)}, u32[]{:S(2)}, u32[]{:S(2)}) collective-permute-start(f32[520,128]{1,0:T(8,128)S(1)} %get-tuple-element.18), channel_id=1, source_target_pairs={{0,1},{1,0},{2,3},{3,2},{4,5},{5,4},{6,7},{7,6},{8,9},{9,8},{10,11... | collective-permute-start | bytes 798728 | tf_op jit(solution)/shard_map/ppermute | solution.py:152
  7.9 0.1 collective-permute-start
  7.9 1.1 %collective-permute-done.1.y = f32[520,128]{1,0:T(8,128)S(1)} collective-permute-done((f32[520,128]{1,0:T(8,128)S(1)}, f32[520,128]{1,0:T(8,128)S(1)}, u32[]{:S(2)}, u32[]{:S(2)}) %collective-permute-start.1) | collective-permute-done | bytes 266272 | tf_op jit(solution)/shard_map/ppermute | solution.py:152
  9.1 0.3 collective-permute-done.y
  9.4 0.7 %join.2 = f32[520,128]{1,0:T(8,128)} custom-call(f32[520,128]{1,0:T(8,128)S(1)} %get-tuple-element.15.x, f32[520,128]{1,0:T(8,128)S(1)} %collective-permute-done.y), custom_call_target="tpu_custom_call" | custom-call | tf_op jit(solution)/shard_map/join/pallas_call | solution.py:141
  10.2 0.0 copy-start.1
  10.2 0.0 copy-start.2
  10.2 2.9 %collective-permute-start.5 = (f32[520,128]{1,0:T(8,128)}, f32[520,128]{1,0:T(8,128)S(1)}, u32[]{:S(2)}, u32[]{:S(2)}) collective-permute-start(f32[520,128]{1,0:T(8,128)} %join.2), channel_id=1, source_target_pairs={{0,2},{1,3},{2,0},{3,1},{4,6},{5,7},{6,4},{7,5},{8,10},{9,11},{10,... | collective-permute-start | bytes 798728 | tf_op jit(solution)/shard_map/ppermute | solution.py:157
  13.0 0.0 collective-permute-start.4
  13.1 6.7 %shard_map.78 = (f32[520,128]{1,0:T(8,128)}, f32[520,128]{1,0:T(8,128)}, f32[1032,128]{1,0:T(8,128)S(1)}) custom-call(s32[96]{0:T(128)} %counts.2, s32[16,96]{1,0:T(8,128)} %pattern.3, bf16[96,256,256]{2,1,0:T(8,128)(2,1)} %rows.3), custom_call_target="tpu_custom_call" | custom-call | tf_op jit(solution)/shard_map/pallas_call | solution.py:119
  19.8 0.1 collective-permute-start.2
  19.9 0.4 collective-permute-start.3
  20.4 0.0 copy-done
  20.4 0.1 collective-permute-done.5.rest_4_
  20.5 5.4 %collective-permute-done.4.rest_3_ = f32[520,128]{1,0:T(8,128)S(1)} collective-permute-done((f32[520,128]{1,0:T(8,128)S(1)}, f32[520,128]{1,0:T(8,128)S(1)}, u32[]{:S(2)}, u32[]{:S(2)}) %collective-permute-start.4) | collective-permute-done | bytes 266272 | tf_op jit(solution)/shard_map/ppermute | solution.py:157
  25.9 0.0 collective-permute-done.2.rest_1_
  25.9 0.0 collective-permute-done.3.rest_2_
  25.9 0.0 copy-done.1
  25.9 0.0 copy-done.2
  25.9 21.8 %finish.1 = (f32[4,192,256]{2,1,0:T(8,128)S(1)}, f32[64,64]{1,0:T(8,128)S(1)}) custom-call(f32[4]{0:T(128)S(1)} %copy-done.1, bf16[4,192,192]{2,1,0:T(8,128)(2,1)S(1)} %constant_dynamic-slice_fusion.sens, f32[1,64]{1,0:T(1,128)S(1)} %bitcast.1, f32[1032,128]{1,0:T(8,128)S(1)} %get-tuple-element.21.rest_0_, f32[520,128]{1,0:T(8,128)S(1)} %collective-permute-done.2.rest_1_, ...), custom_call_target="tpu_custom_call" | custom-call | tf_op jit(solution)/shard_map/finish/pallas_call | solution.py:377
  47.7 0.9 %emit.1 = (f32[4,192,256]{2,1,0:T(8,128)}, f32[64,64]{1,0:T(8,128)}) custom-call(f32[4,192,256]{2,1,0:T(8,128)S(1)} %get-tuple-element.26.rows, f32[64,64]{1,0:T(8,128)S(1)} %get-tuple-element.27.factor), custom_call_target="tpu_custom_call" | custom-call | tf_op jit(solution)/shard_map/emit/pallas_call | solution.py:421
  (2 shorter events, 0.1 us)
Async XLA Ops:
  0.6 19.7 %copy-start = (bf16[16,192,192]{2,1,0:T(8,128)(2,1)S(1)}, bf16[16,192,192]{2,1,0:T(8,128)(2,1)}, u32[]{:S(2)}) copy-start(bf16[16,192,192]{2,1,0:T(8,128)(2,1)} %param.9) | copy-start | bytes 3538948
  6.2 2.8 %collective-permute-start.1 = (f32[520,128]{1,0:T(8,128)S(1)}, f32[520,128]{1,0:T(8,128)S(1)}, u32[]{:S(2)}, u32[]{:S(2)}) collective-permute-start(f32[520,128]{1,0:T(8,128)S(1)} %get-tuple-element.18), channel_id=1, source_target_pairs={{0,1},{1,0},{2,3},{3,2},{4,5},{5,4},{6,7},{7,6},{8,9},{9,8},{10,11... | collective-permute-start | bytes 798728 | tf_op jit(solution)/shard_map/ppermute | solution.py:152
  7.9 1.5 %collective-permute-start = (f32[520,128]{1,0:T(8,128)S(1)}, f32[520,128]{1,0:T(8,128)S(1)}, u32[]{:S(2)}, u32[]{:S(2)}) collective-permute-start(f32[520,128]{1,0:T(8,128)S(1)} %get-tuple-element.16), channel_id=1, source_target_pairs={{0,1},{1,0},{2,3},{3,2},{4,5},{5,4},{6,7},{7,6},{8,9},{9,8},{10,11... | collective-permute-start | bytes 798728 | tf_op jit(solution)/shard_map/ppermute | solution.py:152
  10.2 15.7 %copy-start.1 = (f32[4]{0:T(128)S(1)}, f32[4]{0:T(128)}, u32[]{:S(2)}) copy-start(f32[4]{0:T(128)} %damping.1) | copy-start | bytes 52
  10.2 15.7 %copy-start.2 = (f32[64]{0:T(128)S(1)}, f32[64]{0:T(128)}, u32[]{:S(2)}) copy-start(f32[64]{0:T(128)} %param.11) | copy-start | bytes 772
  10.2 10.3 %collective-permute-start.5 = (f32[520,128]{1,0:T(8,128)}, f32[520,128]{1,0:T(8,128)S(1)}, u32[]{:S(2)}, u32[]{:S(2)}) collective-permute-start(f32[520,128]{1,0:T(8,128)} %join.2), channel_id=1, source_target_pairs={{0,2},{1,3},{2,0},{3,1},{4,6},{5,7},{6,4},{7,5},{8,10},{9,11},{10,... | collective-permute-start | bytes 798728 | tf_op jit(solution)/shard_map/ppermute | solution.py:157
  13.0 12.8 %collective-permute-start.4 = (f32[520,128]{1,0:T(8,128)S(1)}, f32[520,128]{1,0:T(8,128)S(1)}, u32[]{:S(2)}, u32[]{:S(2)}) collective-permute-start(f32[520,128]{1,0:T(8,128)S(1)} %join.3), channel_id=1, source_target_pairs={{0,2},{1,3},{2,0},{3,1},{4,6},{5,7},{6,4},{7,5},{8,10},{9,11},{10,... | collective-permute-start | bytes 798728 | tf_op jit(solution)/shard_map/ppermute | solution.py:157
  19.8 6.1 %collective-permute-start.2 = (f32[520,128]{1,0:T(8,128)}, f32[520,128]{1,0:T(8,128)S(1)}, u32[]{:S(2)}, u32[]{:S(2)}) collective-permute-start(f32[520,128]{1,0:T(8,128)} %get-tuple-element.22), channel_id=1, source_target_pairs={{0,1},{1,0},{2,3},{3,2},{4,5},{5,4},{6,7},{7,6},{8,9},{9,8},{10,11... | collective-permute-start | bytes 798728 | tf_op jit(solution)/shard_map/ppermute | solution.py:152
  19.9 5.9 %collective-permute-start.3 = (f32[520,128]{1,0:T(8,128)}, f32[520,128]{1,0:T(8,128)S(1)}, u32[]{:S(2)}, u32[]{:S(2)}) collective-permute-start(f32[520,128]{1,0:T(8,128)} %get-tuple-element.23), channel_id=1, source_target_pairs={{0,1},{1,0},{2,3},{3,2},{4,5},{5,4},{6,7},{7,6},{8,9},{9,8},{10,11... | collective-permute-start | bytes 798728 | tf_op jit(solution)/shard_map/ppermute | solution.py:152
